TPU v7x, 256 devices: a whole 4x4x8 slice. The times are simulated.
256 devices in a mesh: gz: 8 (over x, core), gx: 32 (over z, y).
Axes of the slice: x: 4, y: 4, z: 8, core: 2. Of those that a mesh axis runs over, the one named last changes fastest.
Arguments:
- volume: float32 [256, 512, 256], P('gz', 'gx')
- measured: float32 [2, 256, 2048], P(None, 'gz')
- weight_blocks: bfloat16 [64, 128, 128], replicated, may hold values from 0 to 2
- view_order: int32 [2], replicated, may hold values from 0 to 1, each once
- tile_voxel: int32 [2, 8, 16384], P(None, 'gz', 'gx'), may hold values from 0 to 1023
- tile_column: int32 [2, 8, 16384], P(None, 'gz', 'gx'), may hold values from 0 to 15
- tile_block: int32 [2, 8, 16384], P(None, 'gz', 'gx'), may hold values from 0 to 63
- entry_count: int32 [2, 8, 32], P(None, 'gz', 'gx'), may hold values from 1 to 512, as said below
Outputs:
- volume_out: float32 [256, 512, 256], P('gz', 'gx')
Inputs may be any that keep to these rules, and one draw needn't show every extreme that they name: Entries of block (a, c) of view v at or past entry_count[v, a, c] are not used; in every view some block has 512 live entries.
All inputs are finite; a program needn't handle non-finite values.
Results may differ from a plain program's by a relative error of at most 0.0027.
Values may be sent and summed in bfloat16 or wider, within the bound.
A program may use at most 64 MiB of HBM per device.

v0:
```python
import jax
import jax.numpy as jnp
from jax import lax
from jax.sharding import PartitionSpec as P

TV_STEPS = 4
smooth_floor = 0.01
step_gain = 0.25
norm_floor = 1e-06
group_rows = 128


def padded_2(cells, sides, width):
    for axis, dim in sides:
        count = lax.axis_size(axis)
        ends = count - 1
        head = lax.slice_in_dim(cells, 0, width, axis=dim)
        tail = lax.slice_in_dim(cells, cells.shape[dim] - width, cells.shape[dim], axis=dim)
        cells = jnp.concatenate(
            [
                lax.ppermute(tail, axis, [(i, (i + 1) % count) for i in range(ends)]),
                cells,
                lax.ppermute(head, axis, [((i + 1) % count, i) for i in range(ends)]),
            ],
            axis=dim,
        )
    return cells


def tv_grad(padded):
    base_cells = padded[:-1, :-1, :-1]
    diff_z = padded[1:, :-1, :-1] - base_cells
    diff_x = padded[:-1, 1:, :-1] - base_cells
    diff_y = padded[:-1, :-1, 1:] - base_cells
    inverse = lax.rsqrt(diff_z * diff_z + diff_x * diff_x + diff_y * diff_y + smooth_floor)
    flow_z = diff_z * inverse
    flow_x = diff_x * inverse
    flow_y = diff_y * inverse
    flow_all = flow_z + flow_x + flow_y
    return flow_z[:-1, 1:, 1:] + flow_x[1:, :-1, 1:] + flow_y[1:, 1:, :-1] - flow_all[1:, 1:, 1:]


def pad_depth(field):
    return jnp.pad(field, ((0, 0), (0, 0), (1, 1)))


def body(
    volume, measured, weight_blocks, view_order, tile_voxel, tile_column, tile_block, entry_count
):
    depth_z, depth_x, depth_y = volume.shape
    tiles_y = depth_y // group_rows
    tiles_u = measured.shape[2] // group_rows
    slab_tiles = depth_z * tiles_u
    plane_tiles = depth_x * tiles_y
    row_weight = jnp.sum(weight_blocks, axis=2, dtype=jnp.float32)
    col_weight = jnp.sum(weight_blocks, axis=1, dtype=jnp.float32)
    offsets = jnp.arange(group_rows, dtype=jnp.int32)
    current = volume
    for turn_index in range(view_order.shape[0]):
        view_index = view_order[turn_index]
        voxel_list = lax.dynamic_index_in_dim(tile_voxel, view_index, 0, keepdims=False)[0]
        column_list = lax.dynamic_index_in_dim(tile_column, view_index, 0, keepdims=False)[0]
        block_list = lax.dynamic_index_in_dim(tile_block, view_index, 0, keepdims=False)[0]
        live_count = lax.dynamic_index_in_dim(entry_count, view_index, 0, keepdims=False)[0, 0]
        rounds = (live_count + group_rows - 1) // group_rows
        voxel_tiles = current.astype(jnp.bfloat16).reshape(-1, group_rows)

        def gather_group(index):
            begin = index * group_rows
            voxels = lax.dynamic_slice_in_dim(voxel_list, begin, group_rows)
            columns = lax.dynamic_slice_in_dim(column_list, begin, group_rows)
            chosen = lax.dynamic_slice_in_dim(block_list, begin, group_rows)
            weight = (begin + offsets < live_count).astype(jnp.float32)[:, None]
            detector = voxels // plane_tiles * tiles_u + columns
            return (voxels, detector, chosen, weight)

        def forward(index, carry):
            projection, ray_sum = carry
            voxels, detector, chosen, weight = gather_group(index)
            product = jnp.einsum(
                "ejk,ek->ej",
                weight_blocks[chosen],
                voxel_tiles[voxels],
                preferred_element_type=jnp.float32,
            )
            return (
                projection.at[detector].add(product * weight),
                ray_sum.at[detector].add(row_weight[chosen] * weight),
            )

        empty = jnp.zeros((slab_tiles, group_rows), jnp.float32)
        projection, ray_sum = lax.fori_loop(0, rounds, forward, (empty, empty))
        target = lax.dynamic_index_in_dim(measured, view_index, 0, keepdims=False).reshape(
            slab_tiles, group_rows
        )
        projection, ray_sum = (
            lax.psum(projection.astype(jnp.bfloat16), "gx").astype(jnp.float32),
            lax.psum(ray_sum.astype(jnp.bfloat16), "gx").astype(jnp.float32),
        )
        residual = ((target - projection) / (ray_sum + 1.0)).astype(jnp.bfloat16)

        def backward(index, carry):
            change, voxel_sum = carry
            voxels, detector, chosen, weight = gather_group(index)
            product = jnp.einsum(
                "ejk,ej->ek",
                weight_blocks[chosen],
                residual[detector],
                preferred_element_type=jnp.float32,
            )
            return (
                change.at[voxels].add(product * weight),
                voxel_sum.at[voxels].add(col_weight[chosen] * weight),
            )

        blank = jnp.zeros((voxel_tiles.shape[0], group_rows), jnp.float32)
        change, voxel_sum = lax.fori_loop(0, rounds, backward, (blank, blank))
        current = current + (change / (voxel_sum + 1.0)).reshape(current.shape)
    art_volume = jnp.maximum(current, 0.0)
    difference = art_volume - volume
    change_part = jnp.sum(difference * difference)
    change_total = None
    change_total = lax.psum(change_part, ("gz", "gx"))
    smooth = art_volume
    for sweep_index in range(TV_STEPS):
        padded = padded_2(smooth, (("gz", 0), ("gx", 1)), 1)
        slope = tv_grad(pad_depth(padded))
        slope_part = jnp.sum(slope * slope)
        if sweep_index == 0:
            slope_total = lax.psum(slope_part, ("gz", "gx"))
        else:
            slope_total = lax.psum(slope_part, ("gz", "gx"))
        change_total, scale_now = (
            change_total,
            step_gain * jnp.sqrt(change_total) / jnp.sqrt(slope_total + norm_floor),
        )
        smooth = smooth - scale_now * slope
    return smooth


def solution(mesh):
    return jax.shard_map(
        body,
        mesh=mesh,
        in_specs=(
            P("gz", "gx", None),
            P(None, "gz", None),
            P(),
            P(),
            P(None, "gz", "gx"),
            P(None, "gz", "gx"),
            P(None, "gz", "gx"),
            P(None, "gz", "gx"),
        ),
        out_specs=P("gz", "gx", None),
        check_vma=False,
    )
```

profile of v0, /device:TPU:1, one launch (start us, length us, event | category | flops | bytes accessed | tf_op | source)
XLA Modules:
  0.0 943.3 jit_solution(2549535672975663778)
XLA Ops:
  17.6 13.5 %while.60 = (s32[]{:T(128)}, f32[512,128]{1,0:T(8,128)S(1)}, f32[512,128]{1,0:T(8,128)}, s32[]{:T(128)}, s32[512]{0:T(512)S(1)}, /*index=5*/s32[512]{0:T(512)S(1...) while((s32[]{:T(128)}, f32[512,128]{1,0:T(8,128)S(1)}, ...), condition=%wide.region_4.5_spmd.clone, body=%wide.region_1.4_spmd.clone.sunk | while | flops 4265478 | bytes 13388487 | solution.py:92
  21.5 4.4 fusion.99
  36.0 180.4 %all-reduce.12.cloned.1.call-done = (bf16[512,128]{1,0:T(8,128)(2,1)}, bf16[512,128]{1,0:T(8,128)(2,1)}) async-done(((bf16[512,128]{1,0:T(8,128)(2,1)}, bf16[512,128]{1,0:T(8,128)(2,1)}), (bf16[512,128]{1,0:T(8,128)(2,1)}, bf16[512,128]{1,0:T(8,128)(2,1)})) %all-reduce.12.cloned.1.call-update) | async-done | bytes 262160 | tf_op jit(solution)/shard_map/psum | solution.py:98
  219.1 14.2 %while.61 = (s32[]{:T(128)}, f32[1024,128]{1,0:T(8,128)}, f32[1024,128]{1,0:T(8,128)}, s32[]{:T(128)}, s32[512]{0:T(512)S(1)}, /*index=5*/s32[512]{0:T(512)S(1)}...) while((s32[]{:T(128)}, f32[1024,128]{1,0:T(8,128)}, ...), condition=%wide.region_11.12_spmd.clone, body=%wide.region_8.11_spmd.clone.sunk | while | flops 4265478 | bytes 13912775 | solution.py:117
  223.0 3.4 fusion.104
  230.1 3.3 scatter_custom_fusion.47
  241.9 14.9 %while.62 = (s32[]{:T(128)}, f32[512,128]{1,0:T(8,128)}, f32[512,128]{1,0:T(8,128)}, s32[]{:T(128)}, s32[512]{0:T(512)S(1)}, /*index=5*/s32[512]{0:T(512)S(1)}, ...) while((s32[]{:T(128)}, f32[512,128]{1,0:T(8,128)}, ...), condition=%wide.region_15.16_spmd.clone, body=%wide.region_12.15_spmd.clone.sunk | while | flops 4265478 | bytes 13388487 | solution.py:92
  245.7 4.4 fusion.109
  260.8 227.2 %all-reduce.10.cloned.1.call-done = (bf16[512,128]{1,0:T(8,128)(2,1)}, bf16[512,128]{1,0:T(8,128)(2,1)}) async-done(((bf16[512,128]{1,0:T(8,128)(2,1)}, bf16[512,128]{1,0:T(8,128)(2,1)}), (bf16[512,128]{1,0:T(8,128)(2,1)}, bf16[512,128]{1,0:T(8,128)(2,1)})) %all-reduce.10.cloned.1.call-update) | async-done | bytes 262160 | tf_op jit(solution)/shard_map/psum | solution.py:98
  490.0 12.7 %while.63 = (s32[]{:T(128)}, f32[1024,128]{1,0:T(8,128)S(1)}, f32[1024,128]{1,0:T(8,128)}, s32[]{:T(128)}, s32[512]{0:T(512)S(1)}, /*index=5*/s32[512]{0:T(512)S...) while((s32[]{:T(128)}, f32[1024,128]{1,0:T(8,128)S(1)}, ...), condition=%wide.region_21.22_spmd.clone, body=%wide.region_18.21_spmd.clone.sunk | while | flops 4265478 | bytes 13912775 | solution.py:117
  493.8 3.4 fusion.114
  499.4 3.3 scatter_custom_fusion.55
  504.9 8.1 collective-permute-start
  521.3 3.4 collective-permute-done.3
  527.9 113.9 %all-reduce.4 = (f32[]{:T(128)}, f32[]{:T(128)}) all-reduce(f32[]{:T(128)} %get-tuple-element.839, f32[]{:T(128)} %get-tuple-element.837), channel_id=1, replica_groups=mesh['gz'=8,'gx'=32] {'gz','gx'}, use_global_device_ids=true, to_apply=%region_23.24 | all-reduce | flops 2 | bytes 16 | tf_op jit(solution)/shard_map/psum | solution.py:123
  643.4 3.5 collective-permute-start.4
  654.8 3.6 collective-permute-done.7
  661.7 77.6 %psum.69 = f32[]{:T(128)} all-reduce(f32[]{:T(128)} %get-tuple-element.833), channel_id=1, replica_groups=mesh['gz'=8,'gx'=32] {'gz','gx'}, use_global_device_ids=true, to_apply=%region_27.28 | all-reduce | flops 1 | bytes 8 | tf_op jit(solution)/shard_map/psum | solution.py:132
  740.1 3.5 collective-permute-start.8
  751.6 3.4 collective-permute-done.11
  758.3 78.8 %psum.70 = f32[]{:T(128)} all-reduce(f32[]{:T(128)} %get-tuple-element.829), channel_id=1, replica_groups=mesh['gz'=8,'gx'=32] {'gz','gx'}, use_global_device_ids=true, to_apply=%region_29.30 | all-reduce | flops 1 | bytes 8 | tf_op jit(solution)/shard_map/psum | solution.py:132
  837.8 3.5 collective-permute-start.12
  849.2 3.6 collective-permute-done.15
  856.0 78.8 %psum.71 = f32[]{:T(128)} all-reduce(f32[]{:T(128)} %get-tuple-element.825), channel_id=1, replica_groups=mesh['gz'=8,'gx'=32] {'gz','gx'}, use_global_device_ids=true, to_apply=%region_31.32 | all-reduce | flops 1 | bytes 8 | tf_op jit(solution)/shard_map/psum | solution.py:132
  (127 shorter events, 109.4 us)
Async XLA Ops:
  6.5 10.1 %copy-start.1 = (f32[32,16,256]{2,1,0:T(8,128)S(1)}, f32[32,16,256]{2,1,0:T(8,128)}, u32[]{:S(2)}) copy-start(f32[32,16,256]{2,1,0:T(8,128)} %param.16) | copy-start | bytes 1572868
  6.5 209.8 %all-reduce.12.cloned.1.call-start = ((), (), s32[]{:S(2)}) async-start(), calls=%async_computation.1 | async-start | bytes 524288 | tf_op jit(solution)/shard_map/psum | solution.py:98
  14.3 2.6 copy-start.3
  14.3 2.6 copy-start.4
  14.3 3.4 copy-start
  33.4 454.6 %all-reduce.10.cloned.1.call-start = ((), (), s32[]{:S(2)}) async-start(), calls=%async_computation | async-start | bytes 524288 | tf_op jit(solution)/shard_map/psum | solution.py:98
  502.7 1.3 copy-start.2
  504.9 10.0 %collective-permute-start = (f32[1,16,256]{2,1,0:T(8,128)S(1)}, f32[1,16,256]{2,1,0:T(8,128)S(1)}, u32[]{:S(2)}, u32[]{:S(2)}) collective-permute-start(f32[1,16,256]{2,1,0:T(8,128)S(1)} %get-tuple-element.879), channel_id=1, source_target_pairs={{0,32},{32,64},{64,96},{96,128},{128,160},{160,192},{192,224},{1,3... | collective-permute-start | bytes 49160 | tf_op jit(solution)/shard_map/ppermute | solution.py:21
  513.0 5.1 collective-permute-start.1
  518.1 3.3 collective-permute-start.2
  520.0 4.7 collective-permute-start.3
  643.4 5.5 collective-permute-start.4
  647.0 5.1 collective-permute-start.5
  652.1 2.7 collective-permute-start.6
  653.5 4.9 collective-permute-start.7
  740.1 5.4 collective-permute-start.8
  743.6 5.1 collective-permute-start.9
  748.7 2.9 collective-permute-start.10
  750.1 4.9 collective-permute-start.11
  837.8 5.4 collective-permute-start.12
  841.3 5.1 collective-permute-start.13
  846.5 2.7 collective-permute-start.14
  847.9 4.9 collective-permute-start.15
Sparse Core Ops, SparseCore 0:
  33.6 182.7 all-reduce.11
  260.1 227.8 all-reduce.9
where the time goes:
time: 946 us; the launch traced here: 943 us
  waiting for transfers between devices  434 us (46%)
  blocking collectives  349 us (37%)
  other arithmetic  55.2 us (6%)
  starting transfers between devices  37.9 us (4%)
  local copies, waits for them, and re-layouts  28.9 us (3%)
  between operations  22.3 us (2%)
  matrix products  15.6 us (2%)
    psum x2, waiting for transfers between devices, body(): lax.psum(ray_sum.astype(jnp.bfloat16), 'gx').astype(jnp.float32)  408 us
    psum x3, blocking collectives, body(): slope_total = lax.psum(slope_part, ('gz', 'gx'))  235 us
    psum x1, blocking collectives, body(): change_total = lax.psum(change_part, ('gz', 'gx'))  114 us
    ppermute x8, waiting for transfers between devices, padded_2(): lax.ppermute(head, axis, [((i + 1) % count, i) for i in range(ends)])  26.5 us
    ppermute x8, starting transfers between devices, padded_2(): lax.ppermute(tail, axis, [(i, (i + 1) % count) for i in range(ends)])  24.8 us
  transfers between devices with their start and end apart: 18, of which 10 were waited for; matrix products, arithmetic and copies ran while one was open for 0% of the time, Pallas kernels for 0%

commit v1 on v0

--- a/solution.py
+++ b/solution.py
@@ -129,7 +129,8 @@
         if sweep_index == 0:
             slope_total = lax.psum(slope_part, ("gz", "gx"))
         else:
-            slope_total = lax.psum(slope_part, ("gz", "gx"))
+            partial = lax.psum(slope_part, "gz")
+            slope_total = lax.psum(partial, "gx")
         change_total, scale_now = (
             change_total,
             step_gain * jnp.sqrt(change_total) / jnp.sqrt(slope_total + norm_floor),

time: 946 us -> 975 us (1.031)
  the two profiles are of different devices: /device:TPU:1 before, /device:TPU:128 now
where the time goes in v1:
time: 975 us; the launch traced here: 973 us
  waiting for transfers between devices  380 us (39%)
  blocking collectives  368 us (38%)
  other arithmetic  79.5 us (8%)
  starting transfers between devices  47.7 us (5%)
  local copies, waits for them, and re-layouts  43.7 us (4%)
  matrix products  31.2 us (3%)
  between operations  22.5 us (2%)
    psum x2, waiting for transfers between devices, body(): lax.psum(ray_sum.astype(jnp.bfloat16), 'gx').astype(jnp.float32)  364 us
    psum x3, blocking collectives, body(): slope_total = lax.psum(partial, 'gx')  227 us
    psum x1, blocking collectives, body(): change_total = lax.psum(change_part, ('gz', 'gx'))  99 us
    psum x3, blocking collectives, body(): partial = lax.psum(slope_part, 'gz')  42 us
    ppermute x8, starting transfers between devices, padded_2(): lax.ppermute(head, axis, [((i + 1) % count, i) for i in range(ends)])  33.9 us
  transfers between devices with their start and end apart: 18, of which 10 were waited for; matrix products, arithmetic and copies ran while one was open for 0% of the time, Pallas kernels for 0%

profile of v1, /device:TPU:128, one launch (start us, length us, event | category | flops | bytes accessed | tf_op | source)
XLA Modules:
  0.0 972.5 jit_solution(3804444494537859354)
XLA Ops:
  18.0 27.0 %while.60 = (s32[]{:T(128)}, f32[512,128]{1,0:T(8,128)S(1)}, f32[512,128]{1,0:T(8,128)}, s32[]{:T(128)}, s32[512]{0:T(512)S(1)}, /*index=5*/s32[512]{0:T(512)S(1...) while((s32[]{:T(128)}, f32[512,128]{1,0:T(8,128)S(1)}, ...), condition=%wide.region_4.5_spmd.clone, body=%wide.region_1.4_spmd.clone.sunk | while | flops 4265478 | bytes 13388487 | solution.py:92
  21.8 4.4 fusion.99
  35.3 4.4 fusion.99
  49.7 166.2 %all-reduce.12.cloned.1.call-done = (bf16[512,128]{1,0:T(8,128)(2,1)}, bf16[512,128]{1,0:T(8,128)(2,1)}) async-done(((bf16[512,128]{1,0:T(8,128)(2,1)}, bf16[512,128]{1,0:T(8,128)(2,1)}), (bf16[512,128]{1,0:T(8,128)(2,1)}, bf16[512,128]{1,0:T(8,128)(2,1)})) %all-reduce.12.cloned.1.call-update) | async-done | bytes 262160 | tf_op jit(solution)/shard_map/psum | solution.py:98
  218.7 28.4 %while.61 = (s32[]{:T(128)}, f32[1024,128]{1,0:T(8,128)}, f32[1024,128]{1,0:T(8,128)}, s32[]{:T(128)}, s32[512]{0:T(512)S(1)}, /*index=5*/s32[512]{0:T(512)S(1)}...) while((s32[]{:T(128)}, f32[1024,128]{1,0:T(8,128)}, ...), condition=%wide.region_11.12_spmd.clone, body=%wide.region_8.11_spmd.clone.sunk | while | flops 4265478 | bytes 13912775 | solution.py:117
  222.6 3.4 fusion.104
  255.7 29.5 %while.62 = (s32[]{:T(128)}, f32[512,128]{1,0:T(8,128)}, f32[512,128]{1,0:T(8,128)}, s32[]{:T(128)}, s32[512]{0:T(512)S(1)}, /*index=5*/s32[512]{0:T(512)S(1)}, ...) while((s32[]{:T(128)}, f32[512,128]{1,0:T(8,128)}, ...), condition=%wide.region_15.16_spmd.clone, body=%wide.region_12.15_spmd.clone.sunk | while | flops 4265478 | bytes 13388487 | solution.py:92
  259.5 4.4 fusion.109
  274.2 4.4 fusion.109
  289.2 197.8 %all-reduce.10.cloned.1.call-done = (bf16[512,128]{1,0:T(8,128)(2,1)}, bf16[512,128]{1,0:T(8,128)(2,1)}) async-done(((bf16[512,128]{1,0:T(8,128)(2,1)}, bf16[512,128]{1,0:T(8,128)(2,1)}), (bf16[512,128]{1,0:T(8,128)(2,1)}, bf16[512,128]{1,0:T(8,128)(2,1)})) %all-reduce.10.cloned.1.call-update) | async-done | bytes 262160 | tf_op jit(solution)/shard_map/psum | solution.py:98
  489.0 25.1 %while.63 = (s32[]{:T(128)}, f32[1024,128]{1,0:T(8,128)S(1)}, f32[1024,128]{1,0:T(8,128)}, s32[]{:T(128)}, s32[512]{0:T(512)S(1)}, /*index=5*/s32[512]{0:T(512)S...) while((s32[]{:T(128)}, f32[1024,128]{1,0:T(8,128)S(1)}, ...), condition=%wide.region_21.22_spmd.clone, body=%wide.region_18.21_spmd.clone.sunk | while | flops 4265478 | bytes 13912775 | solution.py:117
  492.8 3.4 fusion.114
  518.9 3.5 collective-permute-done.1
  524.5 7.0 collective-permute-start.3
  536.5 99.0 %all-reduce.4 = (f32[]{:T(128)}, f32[]{:T(128)}) all-reduce(f32[]{:T(128)} %get-tuple-element.839, f32[]{:T(128)} %get-tuple-element.837), channel_id=1, replica_groups=mesh['gz'=8,'gx'=32] {'gz','gx'}, use_global_device_ids=true, to_apply=%region_23.24 | all-reduce | flops 2 | bytes 16 | tf_op jit(solution)/shard_map/psum | solution.py:123
  645.0 7.1 collective-permute-start.7
  656.9 14.4 %psum.90 = f32[]{:T(128)} all-reduce(f32[]{:T(128)} %get-tuple-element.833), channel_id=1, replica_groups=mesh['gz'=8,'gx'=32] {'gz'}, use_global_device_ids=true, to_apply=%region_27.28 | all-reduce | flops 1 | bytes 8 | tf_op jit(solution)/shard_map/psum | solution.py:132
  671.3 75.6 %psum.91 = f32[]{:T(128)} all-reduce(f32[]{:T(128)} %psum.90), channel_id=1, replica_groups=mesh['gz'=8,'gx'=32] {'gx'}, use_global_device_ids=true, to_apply=%region_28.29 | all-reduce | flops 1 | bytes 8 | tf_op jit(solution)/shard_map/psum | solution.py:133
  754.0 7.5 collective-permute-start.11
  766.1 13.8 %psum.92 = f32[]{:T(128)} all-reduce(f32[]{:T(128)} %get-tuple-element.829), channel_id=1, replica_groups=mesh['gz'=8,'gx'=32] {'gz'}, use_global_device_ids=true, to_apply=%region_30.31 | all-reduce | flops 1 | bytes 8 | tf_op jit(solution)/shard_map/psum | solution.py:132
  779.9 75.6 %psum.93 = f32[]{:T(128)} all-reduce(f32[]{:T(128)} %psum.92), channel_id=1, replica_groups=mesh['gz'=8,'gx'=32] {'gx'}, use_global_device_ids=true, to_apply=%region_31.32 | all-reduce | flops 1 | bytes 8 | tf_op jit(solution)/shard_map/psum | solution.py:133
  862.6 7.2 collective-permute-start.15
  874.7 13.8 %psum.94 = f32[]{:T(128)} all-reduce(f32[]{:T(128)} %get-tuple-element.825), channel_id=1, replica_groups=mesh['gz'=8,'gx'=32] {'gz'}, use_global_device_ids=true, to_apply=%region_33.34 | all-reduce | flops 1 | bytes 8 | tf_op jit(solution)/shard_map/psum | solution.py:132
  888.5 75.6 %psum.95 = f32[]{:T(128)} all-reduce(f32[]{:T(128)} %psum.94), channel_id=1, replica_groups=mesh['gz'=8,'gx'=32] {'gx'}, use_global_device_ids=true, to_apply=%region_34.35 | all-reduce | flops 1 | bytes 8 | tf_op jit(solution)/shard_map/psum | solution.py:133
  (166 shorter events, 161.5 us)
Async XLA Ops:
  6.5 10.5 %copy-start.1 = (f32[32,16,256]{2,1,0:T(8,128)S(1)}, f32[32,16,256]{2,1,0:T(8,128)}, u32[]{:S(2)}) copy-start(f32[32,16,256]{2,1,0:T(8,128)} %param.16) | copy-start | bytes 1572868
  6.5 209.4 %all-reduce.12.cloned.1.call-start = ((), (), s32[]{:S(2)}) async-start(), calls=%async_computation.1 | async-start | bytes 524288 | tf_op jit(solution)/shard_map/psum | solution.py:98
  14.7 2.6 copy-start.3
  14.7 2.6 copy-start.4
  14.7 3.4 copy-start
  47.3 439.7 %all-reduce.10.cloned.1.call-start = ((), (), s32[]{:S(2)}) async-start(), calls=%async_computation | async-start | bytes 524288 | tf_op jit(solution)/shard_map/psum | solution.py:98
  514.1 1.3 copy-start.2
  516.3 2.6 collective-permute-start
  517.5 4.8 collective-permute-start.1
  522.4 9.2 collective-permute-start.2
  524.5 8.6 collective-permute-start.3
  636.9 3.1 collective-permute-start.4
  638.6 4.2 collective-permute-start.5
  642.9 9.2 collective-permute-start.6
  645.0 8.7 collective-permute-start.7
  747.6 2.6 collective-permute-start.8
  748.9 3.1 collective-permute-start.9
  752.1 9.4 collective-permute-start.10
  754.0 8.8 collective-permute-start.11
  856.3 2.6 collective-permute-start.12
  857.6 3.1 collective-permute-start.13
  860.7 9.2 collective-permute-start.14
  862.6 8.8 collective-permute-start.15
Sparse Core Ops, SparseCore 0:
  47.4 168.5 all-reduce.11
  288.6 198.3 all-reduce.9
